TPU v7x, 512 devices: a whole 4x8x8 slice. The times are simulated.
512 devices in a mesh: expert: 128 (over y_hi, z, x), tensor: 4 (over y_lo, core).
Axes of the slice: x: 4, y: 8 (y_hi: 4, y_lo: 2; y = y_hi * 2 + y_lo), z: 8, core: 2. Of those that a mesh axis runs over, the one named last changes fastest.
Arguments:
- tokens: bfloat16 [4096, 4096], P('expert'), may hold values from -6 to 6
- routes: int32 [4096, 8], P('expert'), may hold values from 0 to 127, all different within a row; in each aligned block of 32 rows (0 to 31, 32 to 63, ...) at most 3 rows name the same one
- route_weights: float32 [4096, 8], P('expert'), may hold values from 0.1 to 1
- learner_weights: bfloat16 [128, 4096, 1536], P(None, 'expert', 'tensor'), may hold values from -5 to 5
Outputs:
- combined: bfloat16 [4096, 1536], P('expert', 'tensor')
- expert_amax: float32 [128], P('expert')
Inputs may be any that keep to these rules, and one draw needn't show every extreme that they name: `routes`: each row names 8 different experts; within the 32 rows of one index of expert no expert is named by more than 3 rows, a bound that some block reaches there.
All inputs are finite; a program needn't handle non-finite values.
Results may differ from a plain program's by a relative error of at most 0.0049.
Values may be sent and summed in bfloat16 or wider, within the bound.
A program may use at most 64 MiB of HBM per device.

v0:
```python
import jax
import jax.numpy as jnp
from jax import lax
from jax.sharding import PartitionSpec as P


def over_pieces(value, axis):
    blocks = lax.all_gather(value, axis)
    return blocks.max(axis=0)


def shards(tokens, routes, route_weights, learner_weights):
    expert_count = lax.axis_size("expert")
    row_count, width = tokens.shape
    choose_count = routes.shape[1]
    capacity = min(row_count, max(2, 3 * row_count * choose_count // (2 * expert_count)))
    flat_ids = routes.reshape(-1)
    one_hot = (flat_ids[:, None] == jnp.arange(expert_count, dtype=jnp.int32)[None, :]).astype(
        jnp.int32
    )
    slot_rank = jnp.sum(jnp.cumsum(one_hot, axis=0) * one_hot, axis=1) - 1
    slot_index = flat_ids * capacity + slot_rank
    token_of = jnp.arange(flat_ids.shape[0], dtype=jnp.int32) // choose_count
    relaid = lax.all_to_all(learner_weights, "expert", split_axis=0, concat_axis=1, tiled=True)
    own_weight = relaid[0]
    local_max = jnp.max(jnp.abs(own_weight)).astype(jnp.float32).reshape(1)
    expert_amax = over_pieces(local_max, "tensor")
    quarter = width // lax.axis_size("tensor")
    columns = lax.dynamic_slice_in_dim(tokens, lax.axis_index("tensor") * quarter, quarter, 1)
    send_buffer = jnp.zeros((expert_count * capacity, quarter), jnp.bfloat16)
    send_buffer = (
        send_buffer.at[slot_index].set(columns[token_of]).reshape(expert_count, capacity, quarter)
    )
    results = jnp.einsum(
        "skd,df->skf",
        lax.all_gather(
            lax.all_to_all(send_buffer, "expert", split_axis=0, concat_axis=0, tiled=True),
            "tensor",
            axis=2,
            tiled=True,
        ),
        own_weight,
        preferred_element_type=jnp.float32,
    ).astype(jnp.bfloat16)
    returned = lax.all_to_all(results, "expert", split_axis=0, concat_axis=0, tiled=True)
    picked = returned.reshape(expert_count * capacity, -1)[slot_index].astype(jnp.float32)
    weighted = (picked * route_weights.reshape(-1, 1)).reshape(row_count, choose_count, -1)
    combined = jnp.sum(weighted, axis=1).astype(jnp.bfloat16)
    return (combined, expert_amax)


def solution(mesh):
    return jax.shard_map(
        shards,
        mesh=mesh,
        in_specs=(
            P("expert", None),
            P("expert", None),
            P("expert", None),
            P(None, "expert", "tensor"),
        ),
        out_specs=(P("expert", "tensor"), P("expert")),
        check_vma=False,
    )
```

profile of v0, /device:TPU:6, one launch (start us, length us, event | category | flops | bytes accessed | tf_op | source)
XLA Modules:
  0.0 218.3 jit_solution(5707397659243009915)
XLA Ops:
  7.2 0.8 copy.16
  8.2 0.7 broadcast_multiply_fusion
  8.9 0.1 copy.18
  9.0 0.2 fusion.4
  9.3 0.2 fusion.5
  9.6 0.1 mul.35
  9.7 3.7 %scatter_custom_fusion = bf16[384,1024]{1,0:T(8,128)(2,1)S(1)} fusion(s32[256]{0:T(256)S(1)} %bitcast.30, bf16[32,1024]{1,0:T(8,128)(2,1)S(1)} %constant_dynamic-slice_fusion, s32[1024]{0:T(1024)S(1)} %pad_clamp_fusion.1, bf16[]{:T(256)} %constant.15.clone.1), kind=kCustom, calls=%fused_computation.5 | custom fusion | bytes 786434 | tf_op jit(solution)/shard_map/scatter | solution.py:32
  13.4 0.5 reshape.121
  13.9 51.9 %all_to_all.19 = bf16[128,3,1024]{2,1,0:T(4,128)(2,1)} all-to-all(bf16[128,3,1024]{2,1,0:T(4,128)(2,1)S(1)} %reshape.121), channel_id=1, replica_groups=mesh['expert'=128,'tensor'=4] {'expert'}, dimensions={0} | all-to-all | bytes 1572864 | tf_op jit(solution)/shard_map/all_to_all | solution.py:37
  65.9 9.3 %all-to-all-start.1 = ((bf16[128,32,384]{2,1,0:T(8,128)(2,1)}), bf16[128,32,384]{2,1,0:T(8,128)(2,1)S(1)}, u32[]{:S(2)}, u32[]{:S(2)}) async-start(bf16[128,32,384]{2,1,0:T(8,128)(2,1)} %param.7), calls=%async_computation.1 | async-start | bytes 6291456 | tf_op jit(solution)/shard_map/all_to_all | solution.py:24
  75.2 2.4 %copy.20 = bf16[128,3,1024]{2,0,1:T(8,128)(2,1)} copy(bf16[128,3,1024]{2,1,0:T(4,128)(2,1)} %all_to_all.19) | data formatting | bytes 1572864 | tf_op jit(solution)/shard_map/all_to_all | solution.py:37
  77.6 96.3 %all-to-all-done.1 = bf16[128,32,384]{2,1,0:T(8,128)(2,1)S(1)} async-done(((bf16[128,32,384]{2,1,0:T(8,128)(2,1)}), bf16[128,32,384]{2,1,0:T(8,128)(2,1)S(1)}, u32[]{:S(2)}, u32[]{:S(2)}) %all-to-all-start.1) | async-done | bytes 3145760 | tf_op jit(solution)/shard_map/all_to_all | solution.py:24
  173.9 3.7 %convolution_convert_fusion = bf16[128,3,384]{2,0,1:T(8,128)(2,1)S(1)} fusion(bf16[128,3,4096]{2,0,1:T(8,128)(2,1)} %all-gather.2.cloned.1.call-done, bf16[4096,384,1]{1,0,2:T(8,128)(2,1)S(1)} %bitcast.26), kind=kOutput, calls=%fused_computation.4 | convolution fusion | flops 1208107008 | bytes 6586368 | tf_op jit(solution)/shard_map/skd,df->skf/dot_general | solution.py:34
  177.6 1.0 copy.21
  178.6 12.9 %all-to-all-start.2 = ((bf16[128,3,384]{2,1,0:T(4,128)(2,1)}), bf16[128,3,384]{2,1,0:T(4,128)(2,1)}, u32[]{:S(2)}, u32[]{:S(2)}) async-start(bf16[128,3,384]{2,1,0:T(4,128)(2,1)} %copy.21), calls=%async_computation.2 | async-start | bytes 786432 | tf_op jit(solution)/shard_map/all_to_all | solution.py:45
  191.5 1.3 dynamic-slice
  192.8 1.0 abs_reduce_fusion
  193.8 1.4 convert_dynamic-update-slice_fusion
  195.2 6.9 %all-reduce = f32[4]{0:T(128)S(1)} all-reduce(f32[4]{0:T(128)S(1)} %convert_dynamic-update-slice_fusion), channel_id=1, replica_groups=mesh['expert'=128,'tensor'=4] {'tensor'}, use_global_device_ids=true, to_apply=%add | all-reduce | flops 4 | bytes 32
  202.1 0.6 reduce.2
  202.7 5.5 %all-to-all-done.2 = bf16[128,3,384]{2,1,0:T(4,128)(2,1)} async-done(((bf16[128,3,384]{2,1,0:T(4,128)(2,1)}), bf16[128,3,384]{2,1,0:T(4,128)(2,1)}, u32[]{:S(2)}, u32[]{:S(2)}) %all-to-all-start.2) | async-done | bytes 294944 | tf_op jit(solution)/shard_map/all_to_all | solution.py:45
  208.2 1.2 reshape.122
  209.5 1.2 gather_fusion
  210.7 0.8 fusion.2
  (24 shorter events, 0.5 us)
Async XLA Ops:
  7.2 2.5 %copy-start = (bf16[32,4096]{1,0:T(8,128)(2,1)S(1)}, bf16[32,4096]{1,0:T(8,128)(2,1)}, u32[]{:S(2)}) copy-start(bf16[32,4096]{1,0:T(8,128)(2,1)} %param.4) | copy-start | bytes 786436
  65.9 108.0 %all-to-all-start.1 = ((bf16[128,32,384]{2,1,0:T(8,128)(2,1)}), bf16[128,32,384]{2,1,0:T(8,128)(2,1)S(1)}, u32[]{:S(2)}, u32[]{:S(2)}) async-start(bf16[128,32,384]{2,1,0:T(8,128)(2,1)} %param.7), calls=%async_computation.1 | async-start | bytes 6291456 | tf_op jit(solution)/shard_map/all_to_all | solution.py:24
  75.1 98.8 %all-gather.2.cloned.1.call-start = ((), (), s32[]{:S(2)}) async-start(), calls=%async_computation.3 | async-start | bytes 3932160 | tf_op jit(solution)/shard_map/all_gather | solution.py:36
  177.6 17.6 %copy-start.1 = (f32[32,8]{0,1:T(8,128)S(1)}, f32[32,8]{0,1:T(8,128)}, u32[]{:S(2)}) copy-start(f32[32,8]{0,1:T(8,128)} %param.6) | copy-start | bytes 3076
  178.6 29.6 %all-to-all-start.2 = ((bf16[128,3,384]{2,1,0:T(4,128)(2,1)}), bf16[128,3,384]{2,1,0:T(4,128)(2,1)}, u32[]{:S(2)}, u32[]{:S(2)}) async-start(bf16[128,3,384]{2,1,0:T(4,128)(2,1)} %copy.21), calls=%async_computation.2 | async-start | bytes 786432 | tf_op jit(solution)/shard_map/all_to_all | solution.py:45
Sparse Core Ops, SparseCore 0:
  78.0 87.3 all-gather.1
where the time goes:
time: 221 us; the launch traced here: 218 us
  waiting for transfers between devices  102 us (46%)
  blocking collectives  58.8 us (27%)
  starting transfers between devices  22.2 us (10%)
  between operations  14.2 us (6%)
  local copies, waits for them, and re-layouts  12.7 us (6%)
  other arithmetic  4.95 us (2%)
  matrix products  3.69 us (2%)
    all_to_all x1, waiting for transfers between devices, shards(): lax.all_to_all(learner_weights, 'expert', split_axis=0, concat_axis=1, ti...  96.3 us
    all_to_all x1, blocking collectives, shards(): lax.all_to_all(send_buffer, 'expert', split_axis=0, concat_axis=0, tiled=...  51.9 us
    all_to_all x1, starting transfers between devices, shards(): lax.all_to_all(results, 'expert', split_axis=0, concat_axis=0, tiled=True)  12.9 us
    all_to_all x1, starting transfers between devices, shards(): lax.all_to_all(learner_weights, 'expert', split_axis=0, concat_axis=1, ti...  9.26 us
    unnamed x1, blocking collectives  6.87 us
    all_to_all x1, waiting for transfers between devices, shards(): lax.all_to_all(results, 'expert', split_axis=0, concat_axis=0, tiled=True)  5.55 us
  transfers between devices with their start and end apart: 3, of which 2 were waited for; matrix products, arithmetic and copies ran while one was open for 3% of the time, Pallas kernels for 0%

commit v1 on v0

v1 whole, which is shorter than its diff:
```python
import jax
import jax.numpy as jnp
from jax import lax
from jax.experimental import pallas as pl
from jax.experimental.pallas import tpu as pltpu
from jax.sharding import PartitionSpec as P

MESH = pl.DeviceIdType.MESH
BF = jnp.bfloat16
F32 = jnp.float32
NX, NZ, NY = 4, 8, 4
EXPERTS, DEPTH, WIDTH, TOP = 128, 32, 384, 8
HALF = 16
LANES = 128
COLS = NY * NZ * HALF


def offset_of(j):
    return jnp.where(j == 0, 2, jnp.where(j == 1, 1, jnp.where(j == 2, 3, 0)))


def kernel(
    tok_ref, route_ref, rw_ref, w_hbm, out_ref, amax_ref,
    w_ref, wt, st, dt, tb, rz, ry, tx, xf, mt, mz, ms, my, mf,
    am_rows, am_send, am_z, am_y, am_x, am_c,
    pf, pa, xa, rl, sl, rs, ss, qb, xb, sz, ao, za, ysa, ysb, ya, yb,
    w_sem, s_tz, r_tz, s_mz, r_mz, s_ty, r_ty, s_my, r_my, s_tx, r_tx, s_mx, r_mx, s_tc, r_tc,
    s_az, r_az, s_ay, r_ay, s_ax, r_ax, s_ac, r_ac,
    s_xa, r_xa, s_rl, r_rl, s_rs, r_rs, s_xb, r_xb, s_za, r_za, s_ya, r_ya, s_yb, r_yb,
):
    e = lax.axis_index("expert")
    t = lax.axis_index("tensor")
    x = lax.rem(e, NX)
    z = lax.rem(e // NX, NZ)
    y = e // (NX * NZ)
    core = lax.rem(t, 2)
    low = t // 2

    def at(yy, zz, xx):
        return (yy * NZ + zz) * NX + xx

    def zp(o):
        return (at(y, lax.rem(z + o, NZ), x), t)

    def yp(o):
        return (at(lax.rem(y + o, NY), z, x), t)

    def xp(o):
        return (at(y, z, lax.rem(x + o, NX)), t)

    sibling = (e, low * 2 + (1 - core))
    across = (e, (1 - low) * 2 + core)

    def remote(src, dst, ssem, rsem, device):
        return pltpu.make_async_remote_copy(
            src_ref=src, dst_ref=dst, send_sem=ssem, recv_sem=rsem, device_id=device, device_id_type=MESH
        )

    load_w = pltpu.make_async_copy(w_hbm, w_ref, w_sem)
    load_w.start()

    barrier = pltpu.get_barrier_semaphore()
    peers = [zp(o) for o in range(1, NZ)] + [yp(o) for o in range(1, NY)] + [xp(o) for o in range(1, NX)]
    peers += [sibling, across]
    for device in peers:
        pl.semaphore_signal(barrier, inc=1, device_id=device, device_id_type=MESH)

    rows = pl.ds(pl.multiple_of(core * HALF, HALF), HALF)
    for zz in range(NZ):
        for yy in range(NY):
            tb[zz, yy] = tok_ref[rows, (yy * NZ + zz) * LANES:(yy * NZ + zz + 1) * LANES]
    place = (
        lax.broadcasted_iota(jnp.int32, (HALF, LANES), 1)
        == lax.broadcasted_iota(jnp.int32, (HALF, LANES), 0) + z * HALF
    ).astype(F32)
    turn = (((0,), (0,)), ((), ()))
    mt[0:TOP] = lax.dot_general(
        route_ref[rows, :].astype(F32), place, turn, precision=lax.Precision.HIGHEST, preferred_element_type=F32
    )
    mt[TOP:2 * TOP] = lax.dot_general(
        rw_ref[rows, :], place, turn, precision=lax.Precision.HIGHEST, preferred_element_type=F32
    )
    pl.semaphore_wait(barrier, len(peers))

    def tz(o):
        return remote(tb.at[lax.rem(z + o, NZ)], rz.at[z], s_tz.at[o - 1], r_tz.at[o - 1], zp(o))

    def tz_in(o):
        return remote(tb.at[z], rz.at[lax.rem(z + NZ - o, NZ)], s_tz.at[o - 1], r_tz.at[o - 1], zp(o))

    def mzc(o):
        return remote(mt, mz.at[o - 1], s_mz.at[o - 1], r_mz.at[o - 1], zp(o))

    for o in (4, 3, 5, 2, 6, 1, 7):
        mzc(o).start()
        tz(o).start()
    rz[z] = tb[z]

    load_w.wait()

    def turn_w(i, _):
        r = pl.multiple_of(i * 256, 256)
        block = w_ref[pl.ds(r, 256), :]
        wt[:, pl.ds(r, 256)] = block.T
        big = jnp.abs(block)
        big = jnp.maximum(jnp.maximum(big[:, 0:128], big[:, 128:256]), big[:, 256:384])
        am_rows[pl.ds(pl.multiple_of(i * 8, 8), 8), :] = jnp.max(big.astype(F32).reshape(8, DEPTH, LANES), axis=1)
        return 0

    lax.fori_loop(0, 16, turn_w, 0)
    am_send[0] = jnp.max(am_rows[...].T.reshape(16, 8, LANES), axis=0)

    for o in range(1, NZ):
        mzc(o).wait_recv()
    gathered = mt[...]
    for o in range(1, NZ):
        gathered = gathered + mz[o - 1]
    ms[...] = gathered
    my[y] = gathered
    for o in range(1, NZ):
        tz_in(o).wait_recv()

    def tyc(o):
        return remote(rz.at[:, lax.rem(y + o, NY)], ry.at[y], s_ty.at[o - 1], r_ty.at[o - 1], yp(o))

    def ty_in(o):
        return remote(rz.at[:, y], ry.at[lax.rem(y + NY - o, NY)], s_ty.at[o - 1], r_ty.at[o - 1], yp(o))

    def myc(o):
        return remote(ms, my.at[y], s_my.at[o - 1], r_my.at[o - 1], yp(o))

    def my_in(o):
        return remote(ms, my.at[lax.rem(y + NY - o, NY)], s_my.at[o - 1], r_my.at[o - 1], yp(o))

    for o in (2, 1, 3):
        myc(o).start()
        tyc(o).start()
    for zz in range(NZ):
        ry[y, zz] = rz[zz, y]
    for o in range(1, NY):
        my_in(o).wait_recv()
        ty_in(o).wait_recv()

    def mxc(o):
        return remote(my, mf.at[core, x], s_mx.at[o - 1], r_mx.at[o - 1], xp(o))

    def mx_in(o):
        return remote(my, mf.at[core, lax.rem(x + NX - o, NX)], s_mx.at[o - 1], r_mx.at[o - 1], xp(o))

    def txc(o):
        return remote(tx.at[lax.rem(x + o, NX)], xf.at[core, x], s_tx.at[o - 1], r_tx.at[o - 1], xp(o))

    def tx_in(o):
        return remote(tx.at[x], xf.at[core, lax.rem(x + NX - o, NX)], s_tx.at[o - 1], r_tx.at[o - 1], xp(o))

    for o in (2, 1, 3):
        mxc(o).start()
    mf[core, x] = my[...]
    for yy in range(NY):
        turned = ry[yy].reshape(NZ * HALF, LANES).T
        for xx in range(NX):
            tx[xx, :, yy * 128:(yy + 1) * 128] = turned[xx * DEPTH:(xx + 1) * DEPTH, :]
    for o in (2, 1, 3):
        txc(o).start()
    xf[core, x] = tx[x]
    for o in range(1, NX):
        mx_in(o).wait_recv()
        tx_in(o).wait_recv()

    def mcc(h):
        return remote(mf.at[h], mf.at[h], s_tc.at[0], r_tc.at[0], sibling)

    def tcc(h):
        return remote(xf.at[h], xf.at[h], s_tc.at[1], r_tc.at[1], sibling)

    mcc(core).start()
    tcc(core).start()

    def compute(i):
        b = lax.rem(i, 2)
        h = lax.rem(core + b, 2)
        xx = lax.rem(x + offset_of(i // 2), NX)
        ids = lax.broadcasted_iota(jnp.int32, (EXPERTS, LANES), 0).astype(F32)
        for yy in range(NY):
            dense = jnp.zeros((EXPERTS, LANES), F32)
            meta = mf[h, xx, yy]
            for k in range(TOP):
                dense = jnp.where(ids == meta[k:k + 1, :], meta[TOP + k:TOP + k + 1, :], dense)
            dt[:, yy * LANES:(yy + 1) * LANES] = dense
        features = xf[h, xx].astype(F32)

        def spread(g, _):
            for j in range(8):
                row = dt[pl.ds(g * 8 + j, 1), :]
                st[pl.ds(pl.multiple_of(g * 256 + j * DEPTH, DEPTH), DEPTH), :] = (features * row).astype(BF)
            return 0

        lax.fori_loop(0, 16, spread, 0)
        part = jnp.dot(wt[...], st[...], preferred_element_type=F32).T
        for yy in range(NY):
            for zz in range(NZ):
                r = (yy * NZ + zz) * HALF
                pf[i, zz, yy] = part[r:r + HALF, :]

    def xac(j):
        return remote(pa.at[j], xa.at[j], s_xa.at[j], r_xa.at[j], xp(offset_of(j)))

    def ring_long(j, s):
        way = 1 - 2 * lax.rem(j, 2)
        return remote(sl.at[j, s - 1], rl.at[j, s - 1], s_rl.at[j, s - 1], r_rl.at[j, s - 1], zp(way + NZ))

    def ring_short(j, s):
        way = 1 - 2 * lax.rem(j, 2)
        return remote(ss.at[j, s - 1], rs.at[j, s - 1], s_rs.at[j, s - 1], r_rs.at[j, s - 1], zp(NZ - way))

    def ring_step(j, s):
        way = 1 - 2 * lax.rem(j, 2)
        held = pf[2 * j + 1, lax.rem(z + way * (5 - s) + NZ, NZ)]
        if s > 1:
            ring_long(j, s - 1).wait_recv()
            held = held + rl[j, s - 2].astype(F32)
        sl[j, s - 1] = held.astype(BF)
        ring_long(j, s).start()
        if s < 4:
            held = pf[2 * j + 1, lax.rem(z - way * (4 - s) + NZ, NZ)]
            if s > 1:
                ring_short(j, s - 1).wait_recv()
                held = held + rs[j, s - 2].astype(F32)
            ss[j, s - 1] = held.astype(BF)
            ring_short(j, s).start()

    def xbc(j):
        return remote(qb.at[j], xb.at[j], s_xb.at[j], r_xb.at[j], xp(offset_of(j)))

    def ring_end(j):
        ring_long(j, 4).wait_recv()
        ring_short(j, 3).wait_recv()
        qb[j] = pf[2 * j + 1, z] + rl[j, 3].astype(F32) + rs[j, 2].astype(F32)

        @pl.when(j < 3)
        def _():
            xbc(j).start()

    def zac(o):
        return remote(sz.at[lax.rem(z + o, NZ)], za.at[o - 1], s_za.at[o - 1], r_za.at[o - 1], zp(o))

    def azc(o):
        return remote(am_send.at[0], am_z.at[o - 1], s_az.at[o - 1], r_az.at[o - 1], zp(o))

    def ayc(o):
        return remote(am_send.at[1], am_y.at[o - 1], s_ay.at[o - 1], r_ay.at[o - 1], yp(o))

    def axc(o):
        return remote(am_send.at[2], am_x.at[o - 1], s_ax.at[o - 1], r_ax.at[o - 1], xp(o))

    def acc(k):
        return remote(am_send.at[3 + k], am_c.at[k], s_ac.at[k], r_ac.at[k], sibling if k == 0 else across)

    def slot(i, _):
        @pl.when(i == 1)
        def _():
            mcc(1 - core).wait_recv()
            tcc(1 - core).wait_recv()

        @pl.when(i < 8)
        def _():
            compute(i)

        b = lax.rem(i, 2)

        @pl.when((b == 0) & (i < 6))
        def _():
            j = i // 2
            pa[j] = pf[i].astype(BF)
            xac(j).start()

        @pl.when((b == 1) & (i <= 7))
        def _():
            ring_step((i - 1) // 2, 1)

        @pl.when((b == 0) & (i >= 2) & (i <= 8))
        def _():
            ring_step((i - 2) // 2, 2)

        @pl.when((b == 1) & (i >= 3) & (i <= 9))
        def _():
            ring_step((i - 3) // 2, 3)

        @pl.when((b == 0) & (i >= 4) & (i <= 10))
        def _():
            ring_step((i - 4) // 2, 4)

        @pl.when((b == 1) & (i >= 5) & (i <= 11))
        def _():
            ring_end((i - 5) // 2)

        @pl.when(i == 7)
        def _():
            for j in range(3):
                xac(j).wait_recv()
            for zz in range(NZ):
                total = pf[6, zz] + xa[0, zz].astype(F32) + xa[1, zz].astype(F32) + xa[2, zz].astype(F32)
                pf[6, zz] = total
                sz[zz] = total.astype(BF)
            for o in (4, 3, 5, 2, 6, 1, 7):
                zac(o).start()

        @pl.when(i == 0)
        def _():
            for o in range(1, NZ):
                azc(o).start()

        @pl.when(i == 2)
        def _():
            top = am_send[0]
            for o in range(1, NZ):
                azc(o).wait_recv()
                top = jnp.maximum(top, am_z[o - 1])
            am_send[1] = top
            for o in range(1, NY):
                ayc(o).start()

        @pl.when(i == 4)
        def _():
            top = am_send[1]
            for o in range(1, NY):
                ayc(o).wait_recv()
                top = jnp.maximum(top, am_y[o - 1])
            am_send[2] = top
            for o in range(1, NX):
                axc(o).start()

        @pl.when(i == 6)
        def _():
            top = am_send[2]
            for o in range(1, NX):
                axc(o).wait_recv()
                top = jnp.maximum(top, am_x[o - 1])
            am_send[3] = top
            acc(0).start()

        @pl.when(i == 8)
        def _():
            acc(0).wait_recv()
            am_send[4] = jnp.maximum(am_send[3], am_c[0])
            acc(1).start()

        return 0

    lax.fori_loop(0, 12, slot, 0)

    def yac(o):
        return remote(ysa.at[lax.rem(y + o, NY)], ya.at[o - 1], s_ya.at[o - 1], r_ya.at[o - 1], yp(o))

    def ybc(o):
        return remote(ysb.at[lax.rem(y + o, NY)], yb.at[o - 1], s_yb.at[o - 1], r_yb.at[o - 1], yp(o))

    total = pf[6, z]
    for o in range(1, NZ):
        zac(o).wait_recv()
        total = total + za[o - 1].astype(F32)
    ysa[...] = total
    for o in (2, 1, 3):
        yac(o).start()
    total = qb[3]
    for j in range(3):
        xbc(j).wait_recv()
        total = total + xb[j]
    ysb[...] = total
    for o in (2, 1, 3):
        ybc(o).start()

    acc(1).wait_recv()
    top = jnp.max(jnp.maximum(am_send[4], am_c[1]), axis=0, keepdims=True)
    mine = lax.broadcasted_iota(jnp.int32, (1, LANES), 1) == e
    amax_ref[0] = jnp.max(jnp.where(mine, top, 0.0))

    total = ysa[y]
    for o in range(1, NY):
        yac(o).wait_recv()
        total = total + ya[o - 1]
    out_ref[rows, :] = total.astype(BF)
    total = ysb[y]
    for o in range(1, NY):
        ybc(o).wait_recv()
        total = total + yb[o - 1]
    out_ref[pl.ds(pl.multiple_of((1 - core) * HALF, HALF), HALF), :] = total.astype(BF)

    for o in range(1, NZ):
        tz(o).wait_send()
        mzc(o).wait_send()
        azc(o).wait_send()
        zac(o).wait_send()
    for o in range(1, NY):
        tyc(o).wait_send()
        myc(o).wait_send()
        ayc(o).wait_send()
        yac(o).wait_send()
        ybc(o).wait_send()
    for o in range(1, NX):
        txc(o).wait_send()
        mxc(o).wait_send()
        axc(o).wait_send()
    mcc(core).wait_send()
    tcc(core).wait_send()
    for k in range(2):
        acc(k).wait_send()
    for j in range(3):
        xac(j).wait_send()
        xbc(j).wait_send()
    for j in range(4):
        for s in range(1, 5):
            ring_long(j, s).wait_send()
            if s < 4:
                ring_short(j, s).wait_send()


def shards(tokens, routes, route_weights, learner_weights):
    vmem = pl.BlockSpec(memory_space=pltpu.VMEM)
    block = (NY, HALF, WIDTH)

    def dma(*shape):
        return [pltpu.SemaphoreType.DMA(shape), pltpu.SemaphoreType.DMA(shape)]

    combined, amax = pl.pallas_call(
        kernel,
        out_shape=(
            jax.ShapeDtypeStruct((2 * HALF, WIDTH), BF),
            jax.ShapeDtypeStruct((1,), F32),
        ),
        in_specs=[vmem, vmem, vmem, pl.BlockSpec(memory_space=pl.ANY)],
        out_specs=(vmem, pl.BlockSpec(memory_space=pltpu.SMEM)),
        scratch_shapes=[
            pltpu.VMEM((EXPERTS * DEPTH, WIDTH), BF),
            pltpu.VMEM((WIDTH, EXPERTS * DEPTH), BF),
            pltpu.VMEM((EXPERTS * DEPTH, COLS), BF),
            pltpu.VMEM((EXPERTS, COLS), F32),
            pltpu.VMEM((NZ, NY, HALF, LANES), BF),
            pltpu.VMEM((NZ, NY, HALF, LANES), BF),
            pltpu.VMEM((NY, NZ, HALF, LANES), BF),
            pltpu.VMEM((NX, DEPTH, COLS), BF),
            pltpu.VMEM((2, NX, DEPTH, COLS), BF),
            pltpu.VMEM((2 * TOP, LANES), F32),
            pltpu.VMEM((NZ - 1, 2 * TOP, LANES), F32),
            pltpu.VMEM((2 * TOP, LANES), F32),
            pltpu.VMEM((NY, 2 * TOP, LANES), F32),
            pltpu.VMEM((2, NX, NY, 2 * TOP, LANES), F32),
            pltpu.VMEM((EXPERTS, LANES), F32),
            pltpu.VMEM((5, 8, LANES), F32),
            pltpu.VMEM((NZ - 1, 8, LANES), F32),
            pltpu.VMEM((NY - 1, 8, LANES), F32),
            pltpu.VMEM((NX - 1, 8, LANES), F32),
            pltpu.VMEM((2, 8, LANES), F32),
            pltpu.VMEM((8, NZ, *block), F32),
            pltpu.VMEM((3, NZ, *block), BF),
            pltpu.VMEM((3, NZ, *block), BF),
            pltpu.VMEM((4, 4, *block), BF),
            pltpu.VMEM((4, 4, *block), BF),
            pltpu.VMEM((4, 3, *block), BF),
            pltpu.VMEM((4, 3, *block), BF),
            pltpu.VMEM((4, *block), F32),
            pltpu.VMEM((3, *block), F32),
            pltpu.VMEM((NZ, *block), BF),
            pltpu.VMEM(block, F32),
            pltpu.VMEM((NZ - 1, *block), BF),
            pltpu.VMEM(block, F32),
            pltpu.VMEM(block, F32),
            pltpu.VMEM((NY - 1, HALF, WIDTH), F32),
            pltpu.VMEM((NY - 1, HALF, WIDTH), F32),
            pltpu.SemaphoreType.DMA,
            *dma(NZ - 1), *dma(NZ - 1), *dma(NY - 1), *dma(NY - 1), *dma(NX - 1), *dma(NX - 1), *dma(2),
            *dma(NZ - 1), *dma(NY - 1), *dma(NX - 1), *dma(2),
            *dma(3), *dma(4, 4), *dma(4, 3), *dma(3), *dma(NZ - 1), *dma(NY - 1), *dma(NY - 1),
        ],
        compiler_params=pltpu.CompilerParams(
            collective_id=0, has_side_effects=True, vmem_limit_bytes=60 * 2**20
        ),
        name="relay",
    )(tokens, routes, route_weights, learner_weights.reshape(EXPERTS * DEPTH, WIDTH))
    return combined, amax


def solution(mesh):
    return jax.shard_map(
        shards,
        mesh=mesh,
        in_specs=(
            P("expert", None),
            P("expert", None),
            P("expert", None),
            P(None, "expert", "tensor"),
        ),
        out_specs=(P("expert", "tensor"), P("expert")),
        check_vma=False,
    )
```

time: 221 us -> 93.2 us (0.42); the launches traced: 218 us -> 92.9 us
  waiting for transfers between devices: 102 us -> 0 us
  Pallas kernels: 0 us -> 86.4 us
  blocking collectives: 58.8 us -> 0 us
  starting transfers between devices: 22.2 us -> 0 us
  between operations: 14.2 us -> 2.38 us
  local copies, waits for them, and re-layouts: 12.7 us -> 4.08 us
  other arithmetic: 4.95 us -> 0 us
  matrix products: 3.69 us -> 0 us
    all_to_all x2 -> x0, waiting for transfers between devices: 102 us -> none  [the longest x1 96.3 us: shards(): lax.all_to_all(learner_weights, 'expert', split_axis=0, concat_axis=1, ti...]
    pallas_call x0 -> x1, Pallas kernels: none -> 86.4 us  [shards(): pl.pallas_call(kernel, out_shape=(jax.ShapeDtypeStruct((2 * HALF, WIDTH),...]
    all_to_all x1 -> x0, blocking collectives: 51.9 us -> none  [shards(): lax.all_to_all(send_buffer, 'expert', split_axis=0, concat_axis=0, tiled=...]
    all_to_all x2 -> x0, starting transfers between devices: 22.1 us -> none  [the longest x1 12.9 us: shards(): lax.all_to_all(results, 'expert', split_axis=0, concat_axis=0, tiled=True)]
    unnamed x1 -> x0, blocking collectives: 6.87 us -> none
    scatter x1 -> x0, local copies, waits for them, and re-layouts: 3.7 us -> none  [shards(): send_buffer.at[slot_index].set(columns[token_of])]
    dot_general x1 -> x0, matrix products: 3.69 us -> none  [shards(): jnp.einsum('skd,df->skf', lax.all_gather(lax.all_to_all(send_buffer, 'exp...]
    all_to_all x1 -> x0, local copies, waits for them, and re-layouts: 2.4 us -> none  [shards(): lax.all_to_all(send_buffer, 'expert', split_axis=0, concat_axis=0, tiled=...]
  transfers between devices with their start and end apart: 3 -> 0, of which waited for: 2 -> 0; matrix products, arithmetic and copies ran while one was open for 3% -> 0% of each run, Pallas kernels for 0% -> 0%
where the time goes in v1:
time: 93.2 us; the launch traced here: 92.9 us
  Pallas kernels  86.4 us (93%)
  local copies, waits for them, and re-layouts  4.08 us (4%)
  between operations  2.38 us (3%)
    pallas_call x1, Pallas kernels, shards(): pl.pallas_call(kernel, out_shape=(jax.ShapeDtypeStruct((2 * HALF, WIDTH),...  86.4 us
    unnamed x3, local copies, waits for them, and re-layouts  4.08 us

profile of v1, /device:TPU:6, one launch (start us, length us, event | category | flops | bytes accessed | tf_op | source)
XLA Modules:
  0.0 92.9 jit_solution(7566187235176596832)
XLA Ops:
  0.6 1.4 %copy.6.route_ref = s32[32,8]{1,0:T(8,128)} copy(s32[32,8]{0,1:T(8,128)} %param.5) | data formatting | bytes 2048 | tf_op args[1]
  2.0 1.4 %copy.7.rw_ref = f32[32,8]{1,0:T(8,128)} copy(f32[32,8]{0,1:T(8,128)} %param.6) | data formatting | bytes 2048 | tf_op args[2]
  3.4 86.4 %relay.1 = (bf16[32,384]{1,0:T(8,128)(2,1)}, f32[1]{0:T(128)}) custom-call(bf16[32,4096]{1,0:T(8,128)(2,1)} %tok_ref.1, s32[32,8]{1,0:T(8,128)} %copy.6.route_ref, f32[32,8]{1,0:T(8,128)} %copy.7.rw_ref, bf16[4096,384]{1,0:T(8,128)(2,1)} %bitcast.1), custom_call_target="tpu_custom_call" | custom-call | tf_op jit(solution)/shard_map/relay/pallas_call | solution.py:425
  89.8 1.3 %copy.10 = bf16[32,384]{1,0:T(8,128)(2,1)} copy(bf16[32,384]{1,0:T(8,128)(2,1)} %get-tuple-element.4) | data formatting | bytes 49152

commit v2 on v1

v2 whole, which is shorter than its diff:
```python
import jax
import jax.numpy as jnp
from jax import lax
from jax.experimental import pallas as pl
from jax.experimental.pallas import tpu as pltpu
from jax.sharding import PartitionSpec as P

MESH = pl.DeviceIdType.MESH
BF = jnp.bfloat16
F32 = jnp.float32
NX, NZ, NY = 4, 8, 4
EXPERTS, DEPTH, WIDTH, TOP = 128, 32, 384, 8
HALF = 16
LANES = 128
COLS = NY * NZ * HALF


A_HALF = 0
ORDER = ((0, 0), (0, 2), (0, 1), (0, 3), (1, 2), (1, 1), (1, 3), (1, 0))
B_RINGS = ((4, 6, 7, 8, 9), (5, 7, 8, 9, 10), (6, 7, 8, 9, 10), (7, 8, 9, 10, 11))
A_RING = (7, 8, 9, 10, 11)
SECOND = 3
AMAX = (0, 4, 6, 8, 9)
STEPS = 12
FAR_FIRST = (4, 5, 3, 6, 2, 7, 1, 0)
SENT = {2: 0, 1: 1, 3: 2}


def pick(i, values):
    found = jnp.int32(values[0])
    for n, value in enumerate(values[1:]):
        found = jnp.where(i == n + 1, value, found)
    return found


def kernel(
    tok_ref, route_ref, rw_ref, w_hbm, out_ref, amax_ref,
    w_ref, wt, st, dt, tb, rz, ry, tx, xf, mt, mz, ms, my, mf,
    am_rows, am_send, am_z, am_y, am_x, am_c,
    pf, pa, xa, rl, sl, rs, ss, qb, xb, ysa, ysb, ya, yb,
    w_sem, s_tz, r_tz, s_mz, r_mz, s_ty, r_ty, s_my, r_my, s_tx, r_tx, s_mx, r_mx, s_tc, r_tc, s_mc, r_mc,
    s_az, r_az, s_ay, r_ay, s_ax, r_ax, s_ac, r_ac,
    s_xa, r_xa, s_rl, r_rl, s_rs, r_rs, s_xb, r_xb, s_ya, r_ya, s_yb, r_yb,
):
    e = lax.axis_index("expert")
    t = lax.axis_index("tensor")
    x = lax.rem(e, NX)
    z = lax.rem(e // NX, NZ)
    y = e // (NX * NZ)
    core = lax.rem(t, 2)
    low = t // 2

    def at(yy, zz, xx):
        return (yy * NZ + zz) * NX + xx

    def zp(o):
        return (at(y, lax.rem(z + o, NZ), x), t)

    def yp(o):
        return (at(lax.rem(y + o, NY), z, x), t)

    def xp(o):
        return (at(y, z, lax.rem(x + o, NX)), t)

    sibling = (e, low * 2 + (1 - core))
    across = (e, (1 - low) * 2 + core)

    def remote(src, dst, ssem, rsem, device):
        return pltpu.make_async_remote_copy(
            src_ref=src, dst_ref=dst, send_sem=ssem, recv_sem=rsem, device_id=device, device_id_type=MESH
        )

    load_w = pltpu.make_async_copy(w_hbm, w_ref, w_sem)
    load_w.start()

    barrier = pltpu.get_barrier_semaphore()
    peers = [zp(o) for o in range(1, NZ)] + [yp(o) for o in range(1, NY)] + [xp(o) for o in range(1, NX)]
    peers += [sibling, across]
    for device in peers:
        pl.semaphore_signal(barrier, inc=1, device_id=device, device_id_type=MESH)

    rows = pl.ds(pl.multiple_of(core * HALF, HALF), HALF)
    for zz in range(NZ):
        for yy in range(NY):
            tb[zz, yy] = tok_ref[rows, (yy * NZ + zz) * LANES:(yy * NZ + zz + 1) * LANES]
    place = (
        lax.broadcasted_iota(jnp.int32, (2 * HALF, LANES), 1)
        == lax.broadcasted_iota(jnp.int32, (2 * HALF, LANES), 0) + (z - core) * HALF
    ) & (lax.broadcasted_iota(jnp.int32, (2 * HALF, LANES), 1) // HALF == z)
    place = place.astype(F32)
    mt[0:TOP] = jnp.dot(route_ref[...].astype(F32), place, precision=lax.Precision.HIGHEST, preferred_element_type=F32)
    mt[TOP:2 * TOP] = jnp.dot(rw_ref[...], place, precision=lax.Precision.HIGHEST, preferred_element_type=F32)
    pl.semaphore_wait(barrier, len(peers))

    def tz(o):
        return remote(tb.at[lax.rem(z + o, NZ)], rz.at[z], s_tz.at[o - 1], r_tz.at[o - 1], zp(o))

    def tz_in(o):
        return remote(tb.at[z], rz.at[lax.rem(z + NZ - o, NZ)], s_tz.at[o - 1], r_tz.at[o - 1], zp(o))

    def mzc(o):
        return remote(mt, mz.at[o - 1], s_mz.at[o - 1], r_mz.at[o - 1], zp(o))

    def tyc(oy, o):
        zs = lax.rem(z + NZ - o, NZ)
        src = (rz if o else tb).at[zs, lax.rem(y + oy, NY)]
        return remote(src, ry.at[y, zs], s_ty.at[oy - 1, o], r_ty.at[oy - 1, o], yp(oy))

    def ty_in(oy, o):
        zs = lax.rem(z + NZ - o, NZ)
        return remote(tb.at[z, y], ry.at[lax.rem(y + NY - oy, NY), zs], s_ty.at[oy - 1, o], r_ty.at[oy - 1, o], yp(oy))

    def myc(o):
        return remote(ms, my.at[y], s_my.at[o - 1], r_my.at[o - 1], yp(o))

    def my_in(o):
        return remote(ms, my.at[lax.rem(y + NY - o, NY)], s_my.at[o - 1], r_my.at[o - 1], yp(o))

    def mxc(ox, oy):
        ys = lax.rem(y + NY - oy, NY)
        return remote(my.at[ys], mf.at[core, x, ys], s_mx.at[ox - 1, oy], r_mx.at[ox - 1, oy], xp(ox))

    def mx_in(ox, oy):
        ys = lax.rem(y + NY - oy, NY)
        dst = mf.at[core, lax.rem(x + NX - ox, NX), ys]
        return remote(my.at[ys], dst, s_mx.at[ox - 1, oy], r_mx.at[ox - 1, oy], xp(ox))

    def txc(ox, oy):
        ys = lax.rem(y + NY - oy, NY)
        src = tx.at[lax.rem(x + ox, NX), ys]
        return remote(src, xf.at[core, x, ys], s_tx.at[ox - 1, oy], r_tx.at[ox - 1, oy], xp(ox))

    def tx_in(ox, oy):
        ys = lax.rem(y + NY - oy, NY)
        dst = xf.at[core, lax.rem(x + NX - ox, NX), ys]
        return remote(tx.at[x, ys], dst, s_tx.at[ox - 1, oy], r_tx.at[ox - 1, oy], xp(ox))

    def mcc(ox, h):
        part = mf.at[h, lax.rem(x + NX - ox, NX)]
        return remote(part, part, s_mc.at[ox], r_mc.at[ox], sibling)

    def tcc(ox, h):
        part = xf.at[h, lax.rem(x + NX - ox, NX)]
        return remote(part, part, s_tc.at[ox], r_tc.at[ox], sibling)

    for o in (4, 3, 5, 2, 6, 1, 7):
        mzc(o).start()
        tz(o).start()
    for oy in (2, 1, 3):
        tyc(oy, 0).start()
    ry[y, z] = tb[z, y]

    load_w.wait()

    def turn_w(i, _):
        r = pl.multiple_of(i * 256, 256)
        block = w_ref[pl.ds(r, 256), :]
        wt[:, pl.ds(r, 256)] = block.T
        big = jnp.abs(block)
        big = jnp.maximum(jnp.maximum(big[:, 0:128], big[:, 128:256]), big[:, 256:384])
        am_rows[pl.ds(pl.multiple_of(i * 8, 8), 8), :] = jnp.max(big.astype(F32).reshape(8, DEPTH, LANES), axis=1)
        return 0

    lax.fori_loop(0, 16, turn_w, 0)
    am_send[0] = jnp.max(am_rows[...].T.reshape(16, 8, LANES), axis=0)

    gathered = mt[...]
    for o in (1, 7, 2, 6, 3, 5, 4):
        tz_in(o).wait_recv()
        for oy in (2, 1, 3):
            tyc(oy, o).start()
        zs = lax.rem(z + NZ - o, NZ)
        ry[y, zs] = rz[zs, y]
        mzc(o).wait_recv()
        gathered = gathered + mz[o - 1]
    ms[...] = gathered
    my[y] = gathered
    for o in (2, 1, 3):
        myc(o).start()

    for oy in (0, 1, 3, 2):
        ys = lax.rem(y + NY - oy, NY)
        if oy:
            my_in(oy).wait_recv()
            for o in range(NZ):
                ty_in(oy, o).wait_recv()
        for ox in (2, 1, 3):
            mxc(ox, oy).start()
        mf[core, x, ys] = my[ys]
        turned = ry[ys].reshape(NZ * HALF, LANES).T
        for xx in range(NX):
            tx[xx, ys] = turned[xx * DEPTH:(xx + 1) * DEPTH, :]
        for ox in (2, 1, 3):
            txc(ox, oy).start()
        xf[core, x, ys] = tx[x, ys]
    mcc(0, core).start()
    tcc(0, core).start()

    def x_arrived():
        for ox in (1, 3, 2):
            for oy in range(NY):
                mx_in(ox, oy).wait_recv()
                tx_in(ox, oy).wait_recv()
            mcc(ox, core).start()
            tcc(ox, core).start()

    def core_arrived():
        for ox in range(NX):
            mcc(ox, 1 - core).wait_recv()
            tcc(ox, 1 - core).wait_recv()

    def compute(i):
        h = lax.rem(core + pick(i, [half for half, _ in ORDER]), 2)
        xx = lax.rem(x + pick(i, [off for _, off in ORDER]), NX)
        ids = lax.broadcasted_iota(jnp.int32, (EXPERTS, LANES), 0).astype(F32)
        for yy in range(NY):
            dense = jnp.zeros((EXPERTS, LANES), F32)
            meta = mf[h, xx, yy]
            for k in range(TOP):
                dense = jnp.where(ids == meta[k:k + 1, :], meta[TOP + k:TOP + k + 1, :], dense)
            dt[:, yy * LANES:(yy + 1) * LANES] = dense
        features = jnp.concatenate([xf[h, xx, yy] for yy in range(NY)], axis=1).astype(F32)

        for n in range(EXPERTS):
            st[n * DEPTH:(n + 1) * DEPTH, :] = (features * dt[n:n + 1, :]).astype(BF)
        part = jnp.dot(wt[...], st[...], preferred_element_type=F32).T
        for yy in range(NY):
            for zz in range(NZ):
                r = (yy * NZ + zz) * HALF
                pf[i, zz, yy] = part[r:r + HALF, :]

    a_steps = [i for i, (half, _) in enumerate(ORDER) if half == A_HALF]
    b_steps = [i for i, (half, _) in enumerate(ORDER) if half != A_HALF]
    a_own = next(i for i in a_steps if ORDER[i][1] == 0)
    b_own = next(n for n, i in enumerate(b_steps) if ORDER[i][1] == 0)
    ways = (1, -1, 1, -1, 1)

    def xac(off, p):
        k = SENT[off]
        part = pl.ds(4 * p, 4)
        return remote(pa.at[k, part], xa.at[k, part], s_xa.at[k, p], r_xa.at[k, p], xp(off))

    def held_block(j, rel):
        zz = lax.rem(z + rel, NZ)
        if j < 4:
            return pf[b_steps[j], zz]
        r = FAR_FIRST.index(rel)
        return pf[a_own, zz] + xa[0, r].astype(F32) + xa[1, r].astype(F32) + xa[2, r].astype(F32)

    def ring_long(j, s):
        return remote(sl.at[j, s - 1], rl.at[j, s - 1], s_rl.at[j, s - 1], r_rl.at[j, s - 1], zp(NZ + ways[j]))

    def ring_short(j, s):
        return remote(ss.at[j, s - 1], rs.at[j, s - 1], s_rs.at[j, s - 1], r_rs.at[j, s - 1], zp(NZ - ways[j]))

    def xbc(off):
        k = SENT[off]
        j = next(n for n, i in enumerate(b_steps) if ORDER[i][1] == off)
        return remote(qb.at[j], xb.at[k], s_xb.at[k], r_xb.at[k], xp(off))

    def ring_step(j, s):
        if j == 4 and s in (1, 3):
            for off in (1, 3, 2):
                xac(off, s // 2).wait_recv()
        block = held_block(j, (ways[j] * (5 - s)) % NZ)
        if s > 1:
            ring_long(j, s - 1).wait_recv()
            block = block + rl[j, s - 2].astype(F32)
        sl[j, s - 1] = block.astype(BF)
        ring_long(j, s).start()
        if s < 4:
            block = held_block(j, (-ways[j] * (4 - s)) % NZ)
            if s > 1:
                ring_short(j, s - 1).wait_recv()
                block = block + rs[j, s - 2].astype(F32)
            ss[j, s - 1] = block.astype(BF)
            ring_short(j, s).start()

    def ring_end(j):
        ring_long(j, 4).wait_recv()
        ring_short(j, 3).wait_recv()
        qb[j] = held_block(j, 0) + rl[j, 3].astype(F32) + rs[j, 2].astype(F32)
        if j < 4 and ORDER[b_steps[j]][1]:
            xbc(ORDER[b_steps[j]][1]).start()

    def azc(o):
        return remote(am_send.at[0], am_z.at[o - 1], s_az.at[o - 1], r_az.at[o - 1], zp(o))

    def ayc(o):
        return remote(am_send.at[1], am_y.at[o - 1], s_ay.at[o - 1], r_ay.at[o - 1], yp(o))

    def axc(o):
        return remote(am_send.at[2], am_x.at[o - 1], s_ax.at[o - 1], r_ax.at[o - 1], xp(o))

    def acc(k):
        return remote(am_send.at[3 + k], am_c.at[k], s_ac.at[k], r_ac.at[k], sibling if k == 0 else across)

    def amax_stage(n):
        top = am_send[n - 1] if n else None
        for o in range(1, NZ) if n == 1 else range(1, NY) if n == 2 else range(1, NX) if n == 3 else ():
            (azc, ayc, axc)[n - 1](o).wait_recv()
            top = jnp.maximum(top, (am_z, am_y, am_x)[n - 1][o - 1])
        if n == 4:
            acc(0).wait_recv()
            top = jnp.maximum(top, am_c[0])
        if n:
            am_send[n] = top
        if n < 3:
            for o in range(1, (NZ, NY, NX)[n]):
                (azc, ayc, axc)[n](o).start()
        else:
            acc(n - 3).start()

    def after(i):
        if i < 8 and i in a_steps and ORDER[i][1]:
            k = SENT[ORDER[i][1]]
            for r, rel in enumerate(FAR_FIRST):
                pa[k, r] = pf[i, lax.rem(z + rel, NZ)].astype(BF)
                if r == 3:
                    xac(ORDER[i][1], 0).start()
        if i == SECOND:
            for n in a_steps:
                if ORDER[n][1]:
                    xac(ORDER[n][1], 1).start()
        for s in (1, 0, 5, 4, 3, 2):
            if s == 0 and i == 0:
                x_arrived()
            for j, when in enumerate((*B_RINGS, A_RING)):
                if s and when[s - 1] == i:
                    ring_end(j) if s == 5 else ring_step(j, s)
        if i in AMAX:
            amax_stage(AMAX.index(i))

    def step(i, _):
        @pl.when(i == 2)
        def _():
            core_arrived()

        @pl.when(i < 8)
        def _():
            compute(i)

        for n in range(STEPS):
            pl.when(i == n)(lambda n=n: after(n))
        return 0

    lax.fori_loop(0, STEPS, step, 0)

    def yac(o):
        return remote(ysa.at[lax.rem(y + o, NY)], ya.at[o - 1], s_ya.at[o - 1], r_ya.at[o - 1], yp(o))

    def ybc(o):
        return remote(ysb.at[lax.rem(y + o, NY)], yb.at[o - 1], s_yb.at[o - 1], r_yb.at[o - 1], yp(o))

    total = qb[b_own]
    for off in (1, 3, 2):
        xbc(off).wait_recv()
        total = total + xb[SENT[off]]
    ysb[...] = total
    for o in (2, 1, 3):
        ybc(o).start()
    ysa[...] = qb[4]
    for o in (2, 1, 3):
        yac(o).start()

    acc(1).wait_recv()
    top = jnp.max(jnp.maximum(am_send[4], am_c[1]), axis=0, keepdims=True)
    mine = lax.broadcasted_iota(jnp.int32, (1, LANES), 1) == e
    amax_ref[0] = jnp.max(jnp.where(mine, top, 0.0))

    for source, copies, arrived, other in ((ysb, ybc, yb, 1 - A_HALF), (ysa, yac, ya, A_HALF)):
        total = source[y]
        for o in range(1, NY):
            copies(o).wait_recv()
            total = total + arrived[o - 1]
        half = lax.rem(core + other, 2)
        out_ref[pl.ds(pl.multiple_of(half * HALF, HALF), HALF), :] = total.astype(BF)

    for o in range(1, NZ):
        tz(o).wait_send()
        mzc(o).wait_send()
        azc(o).wait_send()
    for oy in range(1, NY):
        for o in range(NZ):
            tyc(oy, o).wait_send()
        myc(oy).wait_send()
        ayc(oy).wait_send()
        yac(oy).wait_send()
        ybc(oy).wait_send()
    for ox in range(1, NX):
        for oy in range(NY):
            txc(ox, oy).wait_send()
            mxc(ox, oy).wait_send()
        axc(ox).wait_send()
        xac(ox, 0).wait_send()
        xac(ox, 1).wait_send()
        xbc(ox).wait_send()
    for ox in range(NX):
        mcc(ox, core).wait_send()
        tcc(ox, core).wait_send()
    for k in range(2):
        acc(k).wait_send()
    for j in range(5):
        for s in range(1, 5):
            ring_long(j, s).wait_send()
            if s < 4:
                ring_short(j, s).wait_send()


def shards(tokens, routes, route_weights, learner_weights):
    vmem = pl.BlockSpec(memory_space=pltpu.VMEM)
    block = (NY, HALF, WIDTH)

    def dma(*shape):
        return [pltpu.SemaphoreType.DMA(shape), pltpu.SemaphoreType.DMA(shape)]

    combined, amax = pl.pallas_call(
        kernel,
        out_shape=(
            jax.ShapeDtypeStruct((2 * HALF, WIDTH), BF),
            jax.ShapeDtypeStruct((1,), F32),
        ),
        in_specs=[vmem, vmem, vmem, pl.BlockSpec(memory_space=pl.ANY)],
        out_specs=(vmem, pl.BlockSpec(memory_space=pltpu.SMEM)),
        scratch_shapes=[
            pltpu.VMEM((EXPERTS * DEPTH, WIDTH), BF),
            pltpu.VMEM((WIDTH, EXPERTS * DEPTH), BF),
            pltpu.VMEM((EXPERTS * DEPTH, COLS), BF),
            pltpu.VMEM((EXPERTS, COLS), F32),
            pltpu.VMEM((NZ, NY, HALF, LANES), BF),
            pltpu.VMEM((NZ, NY, HALF, LANES), BF),
            pltpu.VMEM((NY, NZ, HALF, LANES), BF),
            pltpu.VMEM((NX, NY, DEPTH, LANES), BF),
            pltpu.VMEM((2, NX, NY, DEPTH, LANES), BF),
            pltpu.VMEM((2 * TOP, LANES), F32),
            pltpu.VMEM((NZ - 1, 2 * TOP, LANES), F32),
            pltpu.VMEM((2 * TOP, LANES), F32),
            pltpu.VMEM((NY, 2 * TOP, LANES), F32),
            pltpu.VMEM((2, NX, NY, 2 * TOP, LANES), F32),
            pltpu.VMEM((EXPERTS, LANES), F32),
            pltpu.VMEM((5, 8, LANES), F32),
            pltpu.VMEM((NZ - 1, 8, LANES), F32),
            pltpu.VMEM((NY - 1, 8, LANES), F32),
            pltpu.VMEM((NX - 1, 8, LANES), F32),
            pltpu.VMEM((2, 8, LANES), F32),
            pltpu.VMEM((8, NZ, *block), F32),
            pltpu.VMEM((3, NZ, *block), BF),
            pltpu.VMEM((3, NZ, *block), BF),
            pltpu.VMEM((5, 4, *block), BF),
            pltpu.VMEM((5, 4, *block), BF),
            pltpu.VMEM((5, 3, *block), BF),
            pltpu.VMEM((5, 3, *block), BF),
            pltpu.VMEM((5, *block), F32),
            pltpu.VMEM((3, *block), F32),
            pltpu.VMEM(block, F32),
            pltpu.VMEM(block, F32),
            pltpu.VMEM((NY - 1, HALF, WIDTH), F32),
            pltpu.VMEM((NY - 1, HALF, WIDTH), F32),
            pltpu.SemaphoreType.DMA,
            *dma(NZ - 1), *dma(NZ - 1), *dma(NY - 1, NZ), *dma(NY - 1), *dma(NX - 1, NY), *dma(NX - 1, NY), *dma(NX), *dma(NX),
            *dma(NZ - 1), *dma(NY - 1), *dma(NX - 1), *dma(2),
            *dma(3, 2), *dma(5, 4), *dma(5, 3), *dma(3), *dma(NY - 1), *dma(NY - 1),
        ],
        compiler_params=pltpu.CompilerParams(
            collective_id=0, has_side_effects=True, vmem_limit_bytes=60 * 2**20
        ),
        name="relay",
    )(tokens, routes.T, route_weights.T, learner_weights.reshape(EXPERTS * DEPTH, WIDTH))
    return combined, amax


def solution(mesh):
    return jax.shard_map(
        shards,
        mesh=mesh,
        in_specs=(
            P("expert", None),
            P("expert", None),
            P("expert", None),
            P(None, "expert", "tensor"),
        ),
        out_specs=(P("expert", "tensor"), P("expert")),
        check_vma=False,
    )
```

time: 93.2 us -> 80.8 us (0.87)
  Pallas kernels: 86.4 us -> 76.8 us
  local copies, waits for them, and re-layouts: 4.08 us -> 1.35 us
    pallas_call x1, Pallas kernels: 86.4 us -> 76.8 us  [shards(): pl.pallas_call(kernel, out_shape=(jax.ShapeDtypeStruct((2 * HALF, WIDTH),...]
    unnamed x3 -> x1, local copies, waits for them, and re-layouts: 4.08 us -> 1.35 us
where the time goes in v2:
time: 80.8 us; the launch traced here: 80.5 us
  Pallas kernels  76.8 us (95%)
  between operations  2.4 us (3%)
  local copies, waits for them, and re-layouts  1.35 us (2%)
    pallas_call x1, Pallas kernels, shards(): pl.pallas_call(kernel, out_shape=(jax.ShapeDtypeStruct((2 * HALF, WIDTH),...  76.8 us

profile of v2, /device:TPU:6, one launch (start us, length us, event | category | flops | bytes accessed | tf_op | source)
XLA Modules:
  0.0 80.5 jit_solution(13147900017106230311)
XLA Ops:
  0.6 76.8 %relay.1 = (bf16[32,384]{1,0:T(8,128)(2,1)}, f32[1]{0:T(128)}) custom-call(bf16[32,4096]{1,0:T(8,128)(2,1)} %tok_ref.1, s32[8,32]{1,0:T(8,128)} %bitcast.4, f32[8,32]{1,0:T(8,128)} %bitcast.5, bf16[4096,384]{1,0:T(8,128)(2,1)} %bitcast.3), custom_call_target="tpu_custom_call" | custom-call | tf_op jit(solution)/shard_map/relay/pallas_call | solution.py:417
  77.4 1.3 %copy.8 = bf16[32,384]{1,0:T(8,128)(2,1)} copy(bf16[32,384]{1,0:T(8,128)(2,1)} %get-tuple-element.4) | data formatting | bytes 49152

commit v3 on v2

--- a/solution.py
+++ b/solution.py
@@ -15,15 +15,13 @@
 COLS = NY * NZ * HALF
 
 
-A_HALF = 0
-ORDER = ((0, 0), (0, 2), (0, 1), (0, 3), (1, 2), (1, 1), (1, 3), (1, 0))
-B_RINGS = ((4, 6, 7, 8, 9), (5, 7, 8, 9, 10), (6, 7, 8, 9, 10), (7, 8, 9, 10, 11))
-A_RING = (7, 8, 9, 10, 11)
-SECOND = 3
+ORDER = ((0, 0), (0, 1), (0, 3), (0, 2), (1, 1), (1, 3), (1, 2), (1, 0))
+RINGS = ((3, 5, 6, 7, 8), (6, 7, 8, 9, 10), (6, 7, 8, 9, 10), (7, 8, 9, 10, 11))
+SECOND = (4, 6)
 AMAX = (0, 4, 6, 8, 9)
 STEPS = 12
 FAR_FIRST = (4, 5, 3, 6, 2, 7, 1, 0)
-SENT = {2: 0, 1: 1, 3: 2}
+SENT = {1: 0, 3: 1}
 
 
 def pick(i, values):
@@ -229,23 +227,20 @@
                 r = (yy * NZ + zz) * HALF
                 pf[i, zz, yy] = part[r:r + HALF, :]
 
-    a_steps = [i for i, (half, _) in enumerate(ORDER) if half == A_HALF]
-    b_steps = [i for i, (half, _) in enumerate(ORDER) if half != A_HALF]
-    a_own = next(i for i in a_steps if ORDER[i][1] == 0)
-    b_own = next(n for n, i in enumerate(b_steps) if ORDER[i][1] == 0)
-    ways = (1, -1, 1, -1, 1)
-
-    def xac(off, p):
-        k = SENT[off]
+    ways = (-1, -1, 1, 1)
+
+    def xac(half, off, p):
+        k = 2 * half + SENT[off]
         part = pl.ds(4 * p, 4)
         return remote(pa.at[k, part], xa.at[k, part], s_xa.at[k, p], r_xa.at[k, p], xp(off))
 
     def held_block(j, rel):
-        zz = lax.rem(z + rel, NZ)
-        if j < 4:
-            return pf[b_steps[j], zz]
+        half = j % 2
+        block = pf[ORDER.index((half, 2 if j < 2 else 0)), lax.rem(z + rel, NZ)]
+        if j < 2:
+            return block
         r = FAR_FIRST.index(rel)
-        return pf[a_own, zz] + xa[0, r].astype(F32) + xa[1, r].astype(F32) + xa[2, r].astype(F32)
+        return block + xa[2 * half, r].astype(F32) + xa[2 * half + 1, r].astype(F32)
 
     def ring_long(j, s):
         return remote(sl.at[j, s - 1], rl.at[j, s - 1], s_rl.at[j, s - 1], r_rl.at[j, s - 1], zp(NZ + ways[j]))
@@ -253,15 +248,13 @@
     def ring_short(j, s):
         return remote(ss.at[j, s - 1], rs.at[j, s - 1], s_rs.at[j, s - 1], r_rs.at[j, s - 1], zp(NZ - ways[j]))
 
-    def xbc(off):
-        k = SENT[off]
-        j = next(n for n, i in enumerate(b_steps) if ORDER[i][1] == off)
-        return remote(qb.at[j], xb.at[k], s_xb.at[k], r_xb.at[k], xp(off))
+    def xbc(half):
+        return remote(qb.at[half], xb.at[half], s_xb.at[half], r_xb.at[half], xp(2))
 
     def ring_step(j, s):
-        if j == 4 and s in (1, 3):
-            for off in (1, 3, 2):
-                xac(off, s // 2).wait_recv()
+        if j >= 2 and s in (1, 3):
+            for off in SENT:
+                xac(j % 2, off, s // 2).wait_recv()
         block = held_block(j, (ways[j] * (5 - s)) % NZ)
         if s > 1:
             ring_long(j, s - 1).wait_recv()
@@ -276,12 +269,24 @@
             ss[j, s - 1] = block.astype(BF)
             ring_short(j, s).start()
 
+    def yac(o):
+        return remote(ysa.at[lax.rem(y + o, NY)], ya.at[o - 1], s_ya.at[o - 1], r_ya.at[o - 1], yp(o))
+
+    def ybc(o):
+        return remote(ysb.at[lax.rem(y + o, NY)], yb.at[o - 1], s_yb.at[o - 1], r_yb.at[o - 1], yp(o))
+
     def ring_end(j):
         ring_long(j, 4).wait_recv()
         ring_short(j, 3).wait_recv()
         qb[j] = held_block(j, 0) + rl[j, 3].astype(F32) + rs[j, 2].astype(F32)
-        if j < 4 and ORDER[b_steps[j]][1]:
-            xbc(ORDER[b_steps[j]][1]).start()
+        if j < 2:
+            xbc(j).start()
+            return
+        kept, copies = ((ysa, yac), (ysb, ybc))[j - 2]
+        xbc(j - 2).wait_recv()
+        kept[...] = qb[j] + xb[j - 2]
+        for o in (2, 1, 3):
+            copies(o).start()
 
     def azc(o):
         return remote(am_send.at[0], am_z.at[o - 1], s_az.at[o - 1], r_az.at[o - 1], zp(o))
@@ -312,20 +317,20 @@
             acc(n - 3).start()
 
     def after(i):
-        if i < 8 and i in a_steps and ORDER[i][1]:
-            k = SENT[ORDER[i][1]]
+        if i < 8 and ORDER[i][1] in SENT:
+            half, off = ORDER[i]
             for r, rel in enumerate(FAR_FIRST):
-                pa[k, r] = pf[i, lax.rem(z + rel, NZ)].astype(BF)
+                pa[2 * half + SENT[off], r] = pf[i, lax.rem(z + rel, NZ)].astype(BF)
                 if r == 3:
-                    xac(ORDER[i][1], 0).start()
-        if i == SECOND:
-            for n in a_steps:
-                if ORDER[n][1]:
-                    xac(ORDER[n][1], 1).start()
+                    xac(half, off, 0).start()
+        for half in range(2):
+            if i == SECOND[half]:
+                for off in SENT:
+                    xac(half, off, 1).start()
         for s in (1, 0, 5, 4, 3, 2):
             if s == 0 and i == 0:
                 x_arrived()
-            for j, when in enumerate((*B_RINGS, A_RING)):
+            for j, when in enumerate(RINGS):
                 if s and when[s - 1] == i:
                     ring_end(j) if s == 5 else ring_step(j, s)
         if i in AMAX:
@@ -346,29 +351,12 @@
 
     lax.fori_loop(0, STEPS, step, 0)
 
-    def yac(o):
-        return remote(ysa.at[lax.rem(y + o, NY)], ya.at[o - 1], s_ya.at[o - 1], r_ya.at[o - 1], yp(o))
-
-    def ybc(o):
-        return remote(ysb.at[lax.rem(y + o, NY)], yb.at[o - 1], s_yb.at[o - 1], r_yb.at[o - 1], yp(o))
-
-    total = qb[b_own]
-    for off in (1, 3, 2):
-        xbc(off).wait_recv()
-        total = total + xb[SENT[off]]
-    ysb[...] = total
-    for o in (2, 1, 3):
-        ybc(o).start()
-    ysa[...] = qb[4]
-    for o in (2, 1, 3):
-        yac(o).start()
-
     acc(1).wait_recv()
     top = jnp.max(jnp.maximum(am_send[4], am_c[1]), axis=0, keepdims=True)
     mine = lax.broadcasted_iota(jnp.int32, (1, LANES), 1) == e
     amax_ref[0] = jnp.max(jnp.where(mine, top, 0.0))
 
-    for source, copies, arrived, other in ((ysb, ybc, yb, 1 - A_HALF), (ysa, yac, ya, A_HALF)):
+    for source, copies, arrived, other in ((ysa, yac, ya, 0), (ysb, ybc, yb, 1)):
         total = source[y]
         for o in range(1, NY):
             copies(o).wait_recv()
@@ -392,15 +380,16 @@
             txc(ox, oy).wait_send()
             mxc(ox, oy).wait_send()
         axc(ox).wait_send()
-        xac(ox, 0).wait_send()
-        xac(ox, 1).wait_send()
-        xbc(ox).wait_send()
     for ox in range(NX):
         mcc(ox, core).wait_send()
         tcc(ox, core).wait_send()
     for k in range(2):
         acc(k).wait_send()
-    for j in range(5):
+        xbc(k).wait_send()
+        for off in SENT:
+            xac(k, off, 0).wait_send()
+            xac(k, off, 1).wait_send()
+    for j in range(4):
         for s in range(1, 5):
             ring_long(j, s).wait_send()
             if s < 4:
@@ -444,14 +433,14 @@
             pltpu.VMEM((NX - 1, 8, LANES), F32),
             pltpu.VMEM((2, 8, LANES), F32),
             pltpu.VMEM((8, NZ, *block), F32),
-            pltpu.VMEM((3, NZ, *block), BF),
-            pltpu.VMEM((3, NZ, *block), BF),
-            pltpu.VMEM((5, 4, *block), BF),
-            pltpu.VMEM((5, 4, *block), BF),
-            pltpu.VMEM((5, 3, *block), BF),
-            pltpu.VMEM((5, 3, *block), BF),
-            pltpu.VMEM((5, *block), F32),
-            pltpu.VMEM((3, *block), F32),
+            pltpu.VMEM((4, NZ, *block), BF),
+            pltpu.VMEM((4, NZ, *block), BF),
+            pltpu.VMEM((4, 4, *block), BF),
+            pltpu.VMEM((4, 4, *block), BF),
+            pltpu.VMEM((4, 3, *block), BF),
+            pltpu.VMEM((4, 3, *block), BF),
+            pltpu.VMEM((4, *block), F32),
+            pltpu.VMEM((2, *block), F32),
             pltpu.VMEM(block, F32),
             pltpu.VMEM(block, F32),
             pltpu.VMEM((NY - 1, HALF, WIDTH), F32),
@@ -459,7 +448,7 @@
             pltpu.SemaphoreType.DMA,
             *dma(NZ - 1), *dma(NZ - 1), *dma(NY - 1, NZ), *dma(NY - 1), *dma(NX - 1, NY), *dma(NX - 1, NY), *dma(NX), *dma(NX),
             *dma(NZ - 1), *dma(NY - 1), *dma(NX - 1), *dma(2),
-            *dma(3, 2), *dma(5, 4), *dma(5, 3), *dma(3), *dma(NY - 1), *dma(NY - 1),
+            *dma(4, 2), *dma(4, 4), *dma(4, 3), *dma(2), *dma(NY - 1), *dma(NY - 1),
         ],
         compiler_params=pltpu.CompilerParams(
             collective_id=0, has_side_effects=True, vmem_limit_bytes=60 * 2**20

time: 80.8 us -> 79.4 us (0.983)
  Pallas kernels: 76.8 us -> 75.4 us
    pallas_call x1, Pallas kernels: 76.8 us -> 75.4 us  [shards(): pl.pallas_call(kernel, out_shape=(jax.ShapeDtypeStruct((2 * HALF, WIDTH),...]
where the time goes in v3:
time: 79.4 us; the launch traced here: 79.1 us
  Pallas kernels  75.4 us (95%)
  between operations  2.4 us (3%)
  local copies, waits for them, and re-layouts  1.35 us (2%)
    pallas_call x1, Pallas kernels, shards(): pl.pallas_call(kernel, out_shape=(jax.ShapeDtypeStruct((2 * HALF, WIDTH),...  75.4 us

profile of v3, /device:TPU:6, one launch (start us, length us, event | category | flops | bytes accessed | tf_op | source)
XLA Modules:
  0.0 79.1 jit_solution(9016288103222388169)
XLA Ops:
  0.6 75.4 %relay.1 = (bf16[32,384]{1,0:T(8,128)(2,1)}, f32[1]{0:T(128)}) custom-call(bf16[32,4096]{1,0:T(8,128)(2,1)} %tok_ref.1, s32[8,32]{1,0:T(8,128)} %bitcast.4, f32[8,32]{1,0:T(8,128)} %bitcast.5, bf16[4096,384]{1,0:T(8,128)(2,1)} %bitcast.3), custom_call_target="tpu_custom_call" | custom-call | tf_op jit(solution)/shard_map/relay/pallas_call | solution.py:406
  76.0 1.3 %copy.8 = bf16[32,384]{1,0:T(8,128)(2,1)} copy(bf16[32,384]{1,0:T(8,128)(2,1)} %get-tuple-element.4) | data formatting | bytes 49152
